TPU v7x, 32 devices: a whole 2x2x4 slice. The times are simulated.
32 devices in a mesh: req: 16 (over z, y, x), mlp: 2 (over core).
Axes of the slice: x: 2, y: 2, z: 4, core: 2. Of those that a mesh axis runs over, the one named last changes fastest.
Arguments:
- queries: bfloat16 [16, 256, 1536], P('req'), may hold values from -90 to 90
- cached_key_slots: bfloat16 [16, 8192, 512], P('req', 'mlp'), may hold values from -5 to 5
- cached_value_slots: bfloat16 [16, 8192, 512], P('req', 'mlp'), may hold values from -6 to 6
- new_token_keys: bfloat16 [16, 256, 512], P('req', 'mlp'), may hold values from -5.05 to 5.05
- new_token_values: bfloat16 [16, 256, 512], P('req', 'mlp'), may hold values from -6 to 6
- cache_len: int32 [16], replicated, may hold values from 1 to 8192, 65536 in all
- placing: int32 [16], replicated, may hold values from 0 to 15, each once
- w_gate: bfloat16 [1536, 12288], P('req', 'mlp'), may hold values from -0.15625 to 0.15625
- w_up: bfloat16 [1536, 12288], P('req', 'mlp'), may hold values from -0.15625 to 0.15625
- w_down: bfloat16 [12288, 1536], P('mlp', 'req'), may hold values from -0.0546875 to 0.0546875
Outputs:
- mixed: bfloat16 [16, 256, 1536], P('req', 'mlp')
All inputs are finite; a program needn't handle non-finite values.
Results may differ from a plain program's by a relative error of at most 0.019.
Values may be sent and summed in bfloat16 or wider, within the bound.
A program may use at most 192 MiB of HBM per device.

v0:
```python
import jax
import jax.numpy as jnp
from jax import lax
from jax.sharding import PartitionSpec as P

HEAD_SIZE = 256
QUERY_HEADS = 6
KEY_VALUE_HEADS = 2
score_scale = 0.0625
negative = -1e30


def lookup(table, index):
    positions = jnp.arange(table.shape[0], dtype=jnp.int32)
    return jnp.sum(jnp.where(positions == index, table, 0))


def rms_rows(attended):
    wide = attended.astype(jnp.float32)
    return (wide * lax.rsqrt(jnp.mean(wide * wide, axis=-1, keepdims=True) + 1e-06)).astype(
        jnp.bfloat16
    )


def gathered_weights(weighted, denom_local, w_gate, w_up, w_down):
    token_inputs = weighted.shape[0]
    mlp_index = lax.axis_index("mlp")
    row_count = token_inputs // lax.axis_size("mlp")
    weighted, denom = lax.psum((weighted, denom_local), "mlp")
    attended = (
        (weighted / jnp.transpose(denom, (2, 0, 1))[..., None])
        .reshape(token_inputs, QUERY_HEADS * HEAD_SIZE)
        .astype(jnp.bfloat16)
    )
    normed = rms_rows(attended)
    own_attended = lax.dynamic_slice_in_dim(attended, mlp_index * row_count, row_count, 0)
    gate_sum = jnp.dot(
        normed,
        lax.all_gather(w_gate, "req", axis=0, tiled=True),
        preferred_element_type=jnp.float32,
    )
    upper_sum = jnp.dot(
        normed, lax.all_gather(w_up, "req", axis=0, tiled=True), preferred_element_type=jnp.float32
    )
    hidden = (jax.nn.silu(gate_sum) * upper_sum).astype(jnp.bfloat16)
    partial_down = jnp.dot(
        hidden,
        lax.all_gather(w_down, "req", axis=1, tiled=True),
        preferred_element_type=jnp.float32,
    )
    own_rows = lax.psum_scatter(
        partial_down.astype(jnp.bfloat16), "mlp", scatter_dimension=0, tiled=True
    ).astype(jnp.float32)
    residual = own_attended.astype(jnp.float32)
    return (residual + own_rows).astype(jnp.bfloat16)[None]


def body(
    queries,
    cached_key_slots,
    cached_value_slots,
    new_token_keys,
    new_token_values,
    cache_len,
    placing,
    w_gate,
    w_up,
    w_down,
):
    slot_index = lax.axis_index("req")
    mlp_index = lax.axis_index("mlp")
    mlp_count = lax.axis_size("mlp")
    token_inputs = queries.shape[1]
    request_cache = cached_key_slots.shape[1]
    request_new_tokens = new_token_keys.shape[1]
    query_group_width = QUERY_HEADS // KEY_VALUE_HEADS
    row_count = token_inputs // mlp_count
    request = lookup(placing, slot_index)
    live_len = lookup(cache_len, request)
    query_head_rows = queries[0].reshape(
        token_inputs, KEY_VALUE_HEADS, query_group_width, HEAD_SIZE
    )
    request_keys = cached_key_slots[0].reshape(request_cache, KEY_VALUE_HEADS, HEAD_SIZE)
    request_values = cached_value_slots[0].reshape(request_cache, KEY_VALUE_HEADS, HEAD_SIZE)
    new_key_rows = new_token_keys[0].reshape(request_new_tokens, KEY_VALUE_HEADS, HEAD_SIZE)
    new_value_rows = new_token_values[0].reshape(request_new_tokens, KEY_VALUE_HEADS, HEAD_SIZE)
    cache_pos = mlp_index * request_cache + jnp.arange(request_cache, dtype=jnp.int32)
    cache_live = cache_pos < live_len
    scores_old = (
        jnp.einsum(
            "ngrd,cgd->grnc", query_head_rows, request_keys, preferred_element_type=jnp.float32
        )
        * score_scale
    )
    scores_old = jnp.where(cache_live[None, None, None, :], scores_old, negative)
    fresh_pos = mlp_index * request_new_tokens + jnp.arange(request_new_tokens, dtype=jnp.int32)
    causal = fresh_pos[None, :] <= jnp.arange(token_inputs, dtype=jnp.int32)[:, None]
    scores_new = (
        jnp.einsum(
            "ngrd,mgd->grnm", query_head_rows, new_key_rows, preferred_element_type=jnp.float32
        )
        * score_scale
    )
    scores_new = jnp.where(causal[None, None], scores_new, negative)
    local_top = jnp.maximum(scores_old.max(-1), scores_new.max(-1))
    row_top = lax.pmax(local_top, "mlp")
    expo_old = jnp.exp(scores_old - row_top[..., None])
    expo_new = jnp.exp(scores_new - row_top[..., None])
    denom_local = expo_old.sum(-1) + expo_new.sum(-1)
    probs_old = expo_old.astype(jnp.bfloat16)
    probs_new = expo_new.astype(jnp.bfloat16)
    weighted = jnp.einsum(
        "grnc,cgd->ngrd", probs_old, request_values, preferred_element_type=jnp.float32
    )
    weighted = weighted + jnp.einsum(
        "grnm,mgd->ngrd", probs_new, new_value_rows, preferred_element_type=jnp.float32
    )
    if lax.axis_size("req") > 16:
        return gathered_weights(weighted, denom_local, w_gate, w_up, w_down)
    w_in = jnp.stack([w_gate, w_up])
    w_in = lax.all_to_all(w_in, "req", split_axis=2, concat_axis=1, tiled=True)
    w_in = lax.all_gather(w_in, "mlp", axis=2, tiled=True)
    w_out = lax.all_to_all(w_down, "req", split_axis=0, concat_axis=1, tiled=True)
    w_out = lax.all_gather(w_out, "mlp", axis=0, tiled=True)
    denom_rows = jnp.transpose(denom_local, (2, 0, 1))
    weighted = lax.psum_scatter(weighted, "mlp", scatter_dimension=0, tiled=True)
    denom = lax.psum_scatter(denom_rows, "mlp", scatter_dimension=0, tiled=True)
    attended = (
        (weighted / denom[..., None])
        .reshape(row_count, QUERY_HEADS * HEAD_SIZE)
        .astype(jnp.bfloat16)
    )
    normed = lax.all_gather(rms_rows(attended), "req", axis=0, tiled=True)
    gate_sum = jnp.dot(normed, w_in[0], preferred_element_type=jnp.float32)
    upper_sum = jnp.dot(normed, w_in[1], preferred_element_type=jnp.float32)
    hidden = (jax.nn.silu(gate_sum) * upper_sum).astype(jnp.bfloat16)
    partial_down = jnp.dot(hidden, w_out, preferred_element_type=jnp.float32)
    own_rows = lax.psum_scatter(
        partial_down.astype(jnp.bfloat16), "req", scatter_dimension=0, tiled=True
    ).astype(jnp.float32)
    return (attended.astype(jnp.float32) + own_rows).astype(jnp.bfloat16)[None]


def solution(mesh):
    in_specs = (
        P("req", None, None),
        P("req", "mlp", None),
        P("req", "mlp", None),
        P("req", "mlp", None),
        P("req", "mlp", None),
        P(),
        P(),
        P("req", "mlp"),
        P("req", "mlp"),
        P("mlp", "req"),
    )
    out_specs = P("req", "mlp", None)
    return jax.shard_map(body, mesh=mesh, in_specs=in_specs, out_specs=out_specs, check_vma=False)
```

profile of v0, /device:TPU:0, one launch (start us, length us, event | category | flops | bytes accessed | tf_op | source)
XLA Modules:
  0.0 450.4 jit_solution(2439042109606651874)
XLA Ops:
  6.5 0.0 reduce-scatter.10.cloned.1.call-start
  6.5 0.0 copy-start.4
  6.5 1.4 copy.59
  8.0 0.0 copy-start.8
  8.0 0.0 copy-start.9
  8.0 6.9 %reshape_squeeze.15 = bf16[4096,2,256]{2,1,0:T(2,128)(2,1)} reshape(bf16[1,4096,512]{2,1,0:T(8,128)(2,1)} %param.11) | data formatting | bytes 8388608 | tf_op jit(solution)/shard_map/reshape;squeeze | solution.py:83
  15.0 0.0 copy-done.4
  15.0 0.1 iota_compare_fusion
  15.1 0.0 copy-done.8
  15.1 0.6 fusion.20
  15.7 0.0 copy-done.9
  15.8 1.3 fusion.21
  17.0 0.6 add_compare_fusion
  17.6 12.0 %bitcast_reduce_fusion = (f32[2,3,256]{2,1,0:T(4,128)S(1)}, f32[2,4096,256,3]{2,1,3,0:T(8,128)}) fusion(pred[4096]{0:T(1024)(128)(4,1)S(1)} %add_compare_fusion, bf16[256,2,3,256]{0,3,2,1:T(8,128)(2,1)S(1)} %bitcast.63, bf16[4096,2,256,1]{2,1,0,3:T(2,128)(2,1)} %bitcast.61), kind=kOutput, calls=%fused_computation.1 | convolution fusion | flops 3240098304 | bytes 30156800 | tf_op jit(solution)/shard_map/ngrd,cgd->grnc/dot_general | solution.py:90
  29.6 0.3 fusion.25
  29.8 0.0 copy-start
  29.9 2.6 pmax.7
  32.5 11.5 %fusion.1 = f32[2,3,256]{2,1,0:T(4,128)S(1)} fusion(f32[2,4096,256,3]{2,1,3,0:T(8,128)} %get-tuple-element.8, f32[2,3,256]{2,1,0:T(4,128)S(1)} %pmax.7, pred[4096]{0:T(1024)(128)(4,1)S(1)} %add_compare_fusion), kind=kLoop, calls=%fused_computation.4 | loop fusion | flops 25164288 | bytes 25182208 | tf_op jit(solution)/shard_map/reduce_sum | solution.py:109
  44.0 0.0 copy-done
  44.0 0.1 fusion.12
  44.2 0.8 copy.94
  45.0 0.0 reduce-scatter.10.cloned.1.call-update
  45.0 0.0 copy-done.3
  45.0 1.5 pad_maximum_fusion
  46.5 5.3 %copy.69 = bf16[2,96,6144]{1,0,2:T(2,128)(2,1)} copy(bf16[2,96,6144]{2,1,0:T(8,128)(2,1)S(1)} %pad_maximum_fusion) | data formatting | bytes 4718592 | tf_op jit(solution)/shard_map/stack | solution.py:120
  51.9 8.2 %all-to-all-start = ((bf16[2,96,6144]{1,0,2:T(2,128)(2,1)}), bf16[2,96,6144]{1,0,2:T(2,128)(2,1)S(1)}, u32[]{:S(2)}, u32[]{:S(2)}) async-start(bf16[2,96,6144]{1,0,2:T(2,128)(2,1)} %copy.69), calls=%async_computation.1 | async-start | bytes 6291456 | tf_op jit(solution)/shard_map/all_to_all | solution.py:121
  60.1 0.0 copy-start.5
  60.1 0.0 reduce-scatter.6.cloned.1.call-start
  60.1 6.9 %reshape_squeeze.18 = bf16[4096,2,256]{2,1,0:T(2,128)(2,1)} reshape(bf16[1,4096,512]{2,1,0:T(8,128)(2,1)} %param.12) | data formatting | bytes 8388608 | tf_op jit(solution)/shard_map/reshape;squeeze | solution.py:84
  67.1 0.0 copy-done.5
  67.1 0.0 copy-start.1
  67.1 13.5 %fusion.3 = f32[2,3,256,256]{3,2,1,0:T(8,128)S(1)} fusion(f32[2,4096,256,3]{2,1,3,0:T(8,128)} %get-tuple-element.8, f32[2,3,256]{2,1,0:T(4,128)S(1)} %pmax.7, pred[4096]{0:T(1024)(128)(4,1)S(1)} %add_compare_fusion, bf16[4096,2,256,1]{2,1,0,3:T(2,128)(2,1)} %bitcast.62), kind=kOutput, calls=%fused_computation.6 | convolution fusion | flops 3246391296 | bytes 30943232 | tf_op jit(solution)/shard_map/grnc,cgd->ngrd/dot_general | solution.py:112
  80.6 0.0 copy-done.1
  80.6 1.6 add_bitcast_fusion
  82.2 0.0 reduce-scatter.6.cloned.1.call-update
  82.3 0.0 all-gather.6.cloned.1.call-start
  82.3 38.9 %all-to-all-done = bf16[2,96,6144]{1,0,2:T(2,128)(2,1)S(1)} async-done(((bf16[2,96,6144]{1,0,2:T(2,128)(2,1)}), bf16[2,96,6144]{1,0,2:T(2,128)(2,1)S(1)}, u32[]{:S(2)}, u32[]{:S(2)}) %all-to-all-start) | async-done | bytes 2359328 | tf_op jit(solution)/shard_map/all_to_all | solution.py:121
  121.2 5.5 %copy.91 = bf16[2,96,16,384]{3,1,2,0:T(8,128)(2,1)} copy(bf16[2,96,16,384]{1,0,3,2:T(2,128)(2,1)S(1)} %bitcast.56) | data formatting | bytes 4718592 | tf_op jit(solution)/shard_map/all_to_all | solution.py:121
  126.7 0.0 all-gather.6.cloned.1.call-update
  126.8 0.0 all-gather.4.cloned.1.call-start
  126.8 0.0 reduce-scatter.10.cloned.1.call-done
  126.8 1.0 reshape.52
  127.9 0.1 copy.93
  128.0 1.4 multiply_reduce_fusion
  129.4 0.3 copy.68
  129.7 0.8 multiply_convert_fusion.1
  130.5 0.0 all-gather.4.cloned.1.call-update
  130.5 0.0 all-gather.8.cloned.1.call-start
  130.5 0.0 copy-done.2
  130.5 0.1 copy.109
  130.7 44.9 %all_to_all.37 = bf16[16,384,96]{1,2,0:T(8,128)(2,1)} all-to-all(bf16[16,384,96]{1,2,0:T(8,128)(2,1)S(1)} %bitcast.60), channel_id=1, replica_groups=mesh['req'=16,'mlp'=2] {'req'}, dimensions={0} | all-to-all | bytes 2359296 | tf_op jit(solution)/shard_map/all_to_all | solution.py:123
  175.6 0.0 all-gather.8.cloned.1.call-update
  175.6 0.2 reduce-scatter.8.cloned.1.call-start
  175.9 0.0 all-gather.6.cloned.1.call-done
  175.9 96.7 %all-gather.4.cloned.1.call-done = bf16[2048,1536]{0,1:T(8,128)(2,1)} async-done(((bf16[128,1536]{0,1:T(8,128)(2,1)}), bf16[2048,1536]{0,1:T(8,128)(2,1)}) %all-gather.4.cloned.1.call-update) | async-done | bytes 6291472 | tf_op jit(solution)/shard_map/all_gather | solution.py:133
  272.6 8.3 %fusion.9 = f32[2048,768]{1,0:T(8,128)S(1)} fusion(bf16[2048,1536]{0,1:T(8,128)(2,1)} %all-gather.4.cloned.1.call-done, bf16[2,1536,768]{2,1,0:T(8,128)(2,1)} %all-gather.6.cloned.1.call-done), kind=kOutput, calls=%fused_computation.15 | convolution fusion | flops 4831838208 | bytes 14942208 | tf_op jit(solution)/shard_map/dot_general | solution.py:134
  280.9 0.0 copy-done.6
  280.9 0.0 copy-done.7
  280.9 7.6 %multiply_convert_fusion = bf16[2048,768]{1,0:T(8,128)(2,1)} fusion(f32[2048,768]{1,0:T(8,128)S(1)} %fusion.9, bf16[2048,1536]{0,1:T(8,128)(2,1)S(1)} %copy-done.6, bf16[2,1536,768]{2,1,0:T(8,128)(2,1)S(1)} %copy-done.7), kind=kOutput, calls=%fused_computation.9 | convolution fusion | flops 4841275392 | bytes 18087936 | tf_op jit(solution)/shard_map/dot_general | solution.py:135
  288.5 9.1 %convolution_convert_fusion = bf16[2048,1536]{1,0:T(8,128)(2,1)} fusion(bf16[2048,768]{1,0:T(8,128)(2,1)} %multiply_convert_fusion, bf16[768,1536]{0,1:T(8,128)(2,1)} %all-gather.8.cloned.1.call-done), kind=kOutput, calls=%fused_computation.8 | convolution fusion | flops 4834983936 | bytes 11796480 | tf_op jit(solution)/shard_map/dot_general | solution.py:137
  297.7 0.0 reduce-scatter.8.cloned.1.call-update
  297.7 0.3 copy.73
  298.0 143.7 %reduce-scatter.8.cloned.1.call-done = bf16[128,1536]{1,0:T(8,128)(2,1)} async-done(((bf16[2048,1536]{1,0:T(8,128)(2,1)}), bf16[128,1536]{1,0:T(8,128)(2,1)}) %reduce-scatter.8.cloned.1.call-update) | async-done | bytes 393232 | tf_op jit(solution)/shard_map/reduce_scatter | solution.py:138
  441.7 1.8 fusion.16
  (13 shorter events, 0.1 us)
Async XLA Ops:
  6.5 120.3 %reduce-scatter.10.cloned.1.call-start = ((), (), s32[]{:S(2)}) async-start(), calls=%async_computation.10 | async-start | bytes 196608
  6.5 8.4 %copy-start.4 = (bf16[1,128,512]{2,1,0:T(8,128)(2,1)S(1)}, bf16[1,128,512]{2,1,0:T(8,128)(2,1)}, u32[]{:S(2)}) copy-start(bf16[1,128,512]{2,1,0:T(8,128)(2,1)} %param.13) | copy-start | bytes 393220
  8.0 7.1 %copy-start.8 = (s32[16]{0:T(128)S(1)}, s32[16]{0:T(128)}, u32[]{:S(2)}) copy-start(s32[16]{0:T(128)} %param.16) | copy-start | bytes 196
  8.0 7.8 %copy-start.9 = (s32[16]{0:T(128)S(1)}, s32[16]{0:T(128)}, u32[]{:S(2)}) copy-start(s32[16]{0:T(128)} %param.15) | copy-start | bytes 196
  29.8 14.2 %copy-start = (f32[2,3,256,128]{2,3,1,0:T(8,128)}, f32[2,3,256,128]{2,3,1,0:T(8,128)S(1)}, u32[]{:S(2)}) copy-start(f32[2,3,256,128]{2,3,1,0:T(8,128)S(1)} %get-tuple-element.10) | copy-start | bytes 2359300
  32.5 12.5 %copy-start.3 = (bf16[96,6144]{1,0:T(8,128)(2,1)S(1)}, bf16[96,6144]{1,0:T(8,128)(2,1)}, u32[]{:S(2)}) copy-start(bf16[96,6144]{1,0:T(8,128)(2,1)} %param.18) | copy-start | bytes 3538948
  51.9 69.4 %all-to-all-start = ((bf16[2,96,6144]{1,0,2:T(2,128)(2,1)}), bf16[2,96,6144]{1,0,2:T(2,128)(2,1)S(1)}, u32[]{:S(2)}, u32[]{:S(2)}) async-start(bf16[2,96,6144]{1,0,2:T(2,128)(2,1)} %copy.69), calls=%async_computation.1 | async-start | bytes 6291456 | tf_op jit(solution)/shard_map/all_to_all | solution.py:121
  60.1 7.0 %copy-start.5 = (bf16[1,128,512]{2,1,0:T(8,128)(2,1)S(1)}, bf16[1,128,512]{2,1,0:T(8,128)(2,1)}, u32[]{:S(2)}) copy-start(bf16[1,128,512]{2,1,0:T(8,128)(2,1)} %param.14) | copy-start | bytes 393220
  60.1 67.9 %reduce-scatter.6.cloned.1.call-start = ((), (), s32[]{:S(2)}) async-start(), calls=%async_computation.5 | async-start | bytes 2359296 | tf_op jit(solution)/shard_map/reduce_scatter | solution.py:126
  67.1 13.5 %copy-start.1 = (f32[2,3,256,128]{2,3,1,0:T(8,128)S(1)}, f32[2,3,256,128]{2,3,1,0:T(8,128)}, u32[]{:S(2)}) copy-start(f32[2,3,256,128]{2,3,1,0:T(8,128)} %copy-done) | copy-start | bytes 2359300
  82.3 93.6 %all-gather.6.cloned.1.call-start = ((), (), s32[]{:S(2)}) async-start(), calls=%async_computation.7 | async-start | bytes 7077888 | tf_op jit(solution)/shard_map/all_gather | solution.py:122
  126.7 3.8 copy-start.2
  126.8 145.9 %all-gather.4.cloned.1.call-start = ((), (), s32[]{:S(2)}) async-start(), calls=%async_computation.6 | async-start | bytes 6684672 | tf_op jit(solution)/shard_map/all_gather | solution.py:133
  130.5 158.1 %all-gather.8.cloned.1.call-start = ((), (), s32[]{:S(2)}) async-start(), calls=%async_computation.8 | async-start | bytes 3538944 | tf_op jit(solution)/shard_map/all_gather | solution.py:124
  175.6 266.1 %reduce-scatter.8.cloned.1.call-start = ((), (), s32[]{:S(2)}) async-start(), calls=%async_computation.9 | async-start | bytes 6684672 | tf_op jit(solution)/shard_map/reduce_scatter | solution.py:138
  272.6 8.3 %copy-start.6 = (bf16[2048,1536]{0,1:T(8,128)(2,1)S(1)}, bf16[2048,1536]{0,1:T(8,128)(2,1)}, u32[]{:S(2)}) copy-start(bf16[2048,1536]{0,1:T(8,128)(2,1)} %all-gather.4.cloned.1.call-done) | copy-start | bytes 18874372
  272.6 8.3 %copy-start.7 = (bf16[2,1536,768]{2,1,0:T(8,128)(2,1)S(1)}, bf16[2,1536,768]{2,1,0:T(8,128)(2,1)}, u32[]{:S(2)}) copy-start(bf16[2,1536,768]{2,1,0:T(8,128)(2,1)} %all-gather.6.cloned.1.call-done) | copy-start | bytes 14155780
Sparse Core Ops, SparseCore 0:
  45.1 10.0 reduce-scatter.9
  82.4 10.3 reduce-scatter.5
  126.9 24.3 all-gather.5
  154.2 118.3 all-gather.3
  274.1 9.0 all-gather.7
  297.8 143.8 reduce-scatter.7
where the time goes:
time: 451 us; the launch traced here: 450 us
  waiting for transfers between devices  280 us (62%)
  matrix products  52.4 us (12%)
  blocking collectives  47.6 us (11%)
  local copies, waits for them, and re-layouts  28.9 us (6%)
  other arithmetic  19.7 us (4%)
  between operations  13.7 us (3%)
  starting transfers between devices  8.58 us (2%)
    reduce_scatter x1, waiting for transfers between devices, body(): lax.psum_scatter(partial_down.astype(jnp.bfloat16), 'req', scatter_dimens...  144 us
    all_gather x1, waiting for transfers between devices, body(): normed = lax.all_gather(rms_rows(attended), 'req', axis=0, tiled=True)  96.7 us
    all_to_all x1, blocking collectives, body(): lax.all_to_all(w_down, 'req', split_axis=0, concat_axis=1, tiled=True)  44.9 us
    all_to_all x1, waiting for transfers between devices, body(): w_in = lax.all_to_all(w_in, 'req', split_axis=2, concat_axis=1, tiled=True)  38.9 us
    dot_general x1, matrix products, body(): jnp.einsum('grnc,cgd->ngrd', probs_old, request_values, preferred_element...  13.5 us
    dot_general x1, matrix products, body(): jnp.einsum('ngrd,cgd->grnc', query_head_rows, request_keys, preferred_ele...  12 us
    reduce_sum x2, other arithmetic, body(): denom_local = expo_old.sum(-1) + expo_new.sum(-1)  11.7 us
    dot_general x1, matrix products, body(): partial_down = jnp.dot(hidden, w_out, preferred_element_type=jnp.float32)  9.13 us
  transfers between devices with their start and end apart: 7, of which 3 were waited for; matrix products, arithmetic and copies ran while one was open for 12% of the time, Pallas kernels for 0%

commit v1 on v0

--- a/solution.py
+++ b/solution.py
@@ -130,7 +130,16 @@
         .reshape(row_count, QUERY_HEADS * HEAD_SIZE)
         .astype(jnp.bfloat16)
     )
-    normed = lax.all_gather(rms_rows(attended), "req", axis=0, tiled=True)
+    shard = rms_rows(attended)
+    ways, here = (lax.axis_size("req"), lax.axis_index("req"))
+    grown, reach = (shard, 1)
+    while reach < ways:
+        theirs = lax.ppermute(grown, "req", [(d, d ^ reach) for d in range(ways)])
+        mine_first = jnp.concatenate([grown, theirs], axis=0)
+        theirs_first = jnp.concatenate([theirs, grown], axis=0)
+        grown = jnp.where(here & reach == 0, mine_first, theirs_first)
+        reach = 2 * reach
+    normed = grown
     gate_sum = jnp.dot(normed, w_in[0], preferred_element_type=jnp.float32)
     upper_sum = jnp.dot(normed, w_in[1], preferred_element_type=jnp.float32)
     hidden = (jax.nn.silu(gate_sum) * upper_sum).astype(jnp.bfloat16)

time: 451 us -> 544 us (1.21)
  blocking collectives: 47.6 us -> 162 us
  waiting for transfers between devices: 280 us -> 212 us
  starting transfers between devices: 8.58 us -> 28.1 us
  other arithmetic: 19.7 us -> 30.8 us
  matrix products: 52.4 us -> 61.3 us
  local copies, waits for them, and re-layouts: 28.9 us -> 34.8 us
    all_to_all x1, blocking collectives: 44.9 us -> 159 us  [body(): lax.all_to_all(w_down, 'req', split_axis=0, concat_axis=1, tiled=True)]
    all_gather x1 -> x0, waiting for transfers between devices: 96.7 us -> none  [body(): normed = lax.all_gather(rms_rows(attended), 'req', axis=0, tiled=True)]
    ppermute x0 -> x4, waiting for transfers between devices: none -> 66.8 us  [body(): theirs = lax.ppermute(grown, 'req', [(d, d ^ reach) for d in range(ways)])]
    all_to_all x1, waiting for transfers between devices: 38.9 us -> 0.01 us  [body(): w_in = lax.all_to_all(w_in, 'req', split_axis=2, concat_axis=1, tiled=True)]
    ppermute x0 -> x4, starting transfers between devices: none -> 19.6 us  [body(): theirs = lax.ppermute(grown, 'req', [(d, d ^ reach) for d in range(ways)])]
    dot_general x1, matrix products: 9.13 us -> 21.2 us  [body(): partial_down = jnp.dot(hidden, w_out, preferred_element_type=jnp.float32)]
    select_n x0 -> x3, other arithmetic: none -> 9.8 us  [body(): grown = jnp.where(here & reach == 0, mine_first, theirs_first)]
    dot_general x1 -> x0, matrix products: 8.27 us -> none  [body(): gate_sum = jnp.dot(normed, w_in[0], preferred_element_type=jnp.float32)]
  transfers between devices with their start and end apart: 7 -> 10, of which waited for: 3 -> 4; matrix products, arithmetic and copies ran while one was open for 12% -> 12% of each run, Pallas kernels for 0% -> 0%
where the time goes in v1:
time: 544 us; the launch traced here: 543 us
  waiting for transfers between devices  212 us (39%)
  blocking collectives  162 us (30%)
  matrix products  61.3 us (11%)
  local copies, waits for them, and re-layouts  34.8 us (6%)
  other arithmetic  30.8 us (6%)
  starting transfers between devices  28.1 us (5%)
  between operations  13.3 us (2%)
    all_to_all x1, blocking collectives, body(): lax.all_to_all(w_down, 'req', split_axis=0, concat_axis=1, tiled=True)  159 us
    reduce_scatter x1, waiting for transfers between devices, body(): lax.psum_scatter(partial_down.astype(jnp.bfloat16), 'req', scatter_dimens...  145 us
    ppermute x4, waiting for transfers between devices, body(): theirs = lax.ppermute(grown, 'req', [(d, d ^ reach) for d in range(ways)])  66.8 us
    dot_general x1, matrix products, body(): partial_down = jnp.dot(hidden, w_out, preferred_element_type=jnp.float32)  21.2 us
    ppermute x4, starting transfers between devices, body(): theirs = lax.ppermute(grown, 'req', [(d, d ^ reach) for d in range(ways)])  19.6 us
    dot_general x1, matrix products, body(): jnp.einsum('grnc,cgd->ngrd', probs_old, request_values, preferred_element...  13.5 us
    dot_general x1, matrix products, body(): jnp.einsum('ngrd,cgd->grnc', query_head_rows, request_keys, preferred_ele...  12 us
    dot_general x1, matrix products, body(): upper_sum = jnp.dot(normed, w_in[1], preferred_element_type=jnp.float32)  11.9 us
  transfers between devices with their start and end apart: 10, of which 4 were waited for; matrix products, arithmetic and copies ran while one was open for 12% of the time, Pallas kernels for 0%

profile of v1, /device:TPU:0, one launch (start us, length us, event | category | flops | bytes accessed | tf_op | source)
XLA Modules:
  0.0 542.6 jit_solution(6490281593102442310)
XLA Ops:
  6.5 0.0 reduce-scatter.10.cloned.1.call-start
  6.5 1.4 copy.59
  7.9 0.0 copy-start.2
  8.0 0.0 copy-start.3
  8.0 0.0 copy-start.4
  8.0 7.0 %reshape_squeeze.15 = bf16[4096,2,256]{2,1,0:T(2,128)(2,1)} reshape(bf16[1,4096,512]{2,1,0:T(8,128)(2,1)} %param.11) | data formatting | bytes 8388608 | tf_op jit(solution)/shard_map/reshape;squeeze | solution.py:83
  15.0 0.0 copy-done.2
  15.0 0.1 iota_compare_fusion
  15.1 0.0 copy-done.3
  15.1 0.6 fusion.22
  15.8 1.4 fusion.23
  17.1 0.7 add_compare_fusion
  17.8 12.0 %bitcast_reduce_fusion = (f32[2,3,256]{2,1,0:T(4,128)S(1)}, f32[2,4096,256,3]{2,1,3,0:T(8,128)}) fusion(pred[4096]{0:T(1024)(128)(4,1)S(1)} %add_compare_fusion, bf16[256,2,3,256]{0,3,2,1:T(8,128)(2,1)S(1)} %bitcast.64, bf16[4096,2,256,1]{2,1,0,3:T(2,128)(2,1)} %bitcast.62), kind=kOutput, calls=%fused_computation.1 | convolution fusion | flops 3240098304 | bytes 30156800 | tf_op jit(solution)/shard_map/ngrd,cgd->grnc/dot_general | solution.py:90
  29.8 0.3 fusion.30
  30.1 2.6 pmax.7
  32.7 11.4 %fusion.1 = f32[2,3,256]{2,1,0:T(4,128)S(1)} fusion(f32[2,4096,256,3]{2,1,3,0:T(8,128)} %get-tuple-element.8, f32[2,3,256]{2,1,0:T(4,128)S(1)} %pmax.7, pred[4096]{0:T(1024)(128)(4,1)S(1)} %add_compare_fusion), kind=kLoop, calls=%fused_computation.4 | loop fusion | flops 25164288 | bytes 25182208 | tf_op jit(solution)/shard_map/reduce_sum | solution.py:109
  44.2 0.1 fusion.14
  44.3 0.8 copy.94
  45.1 0.0 reduce-scatter.10.cloned.1.call-update
  45.2 0.0 reduce-scatter.6.cloned.1.call-start
  45.2 6.9 %reshape_squeeze.18 = bf16[4096,2,256]{2,1,0:T(2,128)(2,1)} reshape(bf16[1,4096,512]{2,1,0:T(8,128)(2,1)} %param.12) | data formatting | bytes 8388608 | tf_op jit(solution)/shard_map/reshape;squeeze | solution.py:84
  52.1 13.5 %fusion.3 = f32[2,3,256,256]{3,2,1,0:T(8,128)S(1)} fusion(f32[2,4096,256,3]{2,1,3,0:T(8,128)} %get-tuple-element.8, f32[2,3,256]{2,1,0:T(4,128)S(1)} %pmax.7, pred[4096]{0:T(1024)(128)(4,1)S(1)} %add_compare_fusion, bf16[4096,2,256,1]{2,1,0,3:T(2,128)(2,1)} %bitcast.63), kind=kOutput, calls=%fused_computation.6 | convolution fusion | flops 3246391296 | bytes 30943232 | tf_op jit(solution)/shard_map/grnc,cgd->ngrd/dot_general | solution.py:112
  65.6 0.0 copy-start.1
  65.7 1.7 reshape_squeeze.19
  67.3 2.5 add_bitcast_fusion
  69.8 0.0 reduce-scatter.6.cloned.1.call-update
  69.8 0.0 copy-done.1
  69.9 1.5 pad_maximum_fusion
  71.3 5.3 copy.69
  76.6 8.1 %all-to-all-start = ((bf16[2,96,6144]{1,0,2:T(2,128)(2,1)}), bf16[2,96,6144]{1,0,2:T(2,128)(2,1)S(1)}, u32[]{:S(2)}, u32[]{:S(2)}) async-start(bf16[2,96,6144]{1,0,2:T(2,128)(2,1)} %copy.69), calls=%async_computation.1 | async-start | bytes 6291456 | tf_op jit(solution)/shard_map/all_to_all | solution.py:121
  84.8 0.2 all-gather.3.cloned.1.call-start
  85.0 0.0 reduce-scatter.10.cloned.1.call-done
  85.0 1.0 reshape.52
  86.0 0.1 copy.93
  86.1 2.2 multiply_reduce_fusion
  88.3 2.3 copy.68
  90.6 1.2 multiply_convert_fusion.2
  91.8 2.0 collective-permute-start
  93.8 10.6 %collective-permute-done = bf16[128,1536]{0,1:T(8,128)(2,1)} collective-permute-done((bf16[128,1536]{0,1:T(8,128)(2,1)S(1)}, bf16[128,1536]{0,1:T(8,128)(2,1)}, u32[]{:S(2)}, u32[]{:S(2)}) %collective-permute-start) | collective-permute-done | bytes 393248 | tf_op jit(solution)/shard_map/ppermute | solution.py:137
  104.4 2.2 maximum_select_fusion.5
  106.6 3.9 collective-permute-start.1
  110.5 27.6 %collective-permute-done.1 = bf16[256,1536]{0,1:T(8,128)(2,1)} collective-permute-done((bf16[256,1536]{0,1:T(8,128)(2,1)}, bf16[256,1536]{0,1:T(8,128)(2,1)}, u32[]{:S(2)}, u32[]{:S(2)}) %collective-permute-start.1) | collective-permute-done | bytes 786464 | tf_op jit(solution)/shard_map/ppermute | solution.py:137
  138.1 3.5 maximum_select_fusion.2
  141.5 5.7 %collective-permute-start.2 = (bf16[512,1536]{0,1:T(8,128)(2,1)}, bf16[512,1536]{0,1:T(8,128)(2,1)}, u32[]{:S(2)}, u32[]{:S(2)}) collective-permute-start(bf16[512,1536]{0,1:T(8,128)(2,1)} %maximum_select_fusion.2), channel_id=1, source_target_pairs={{0,8},{2,10},{4,12},{6,14},{8,0},{10,2},{12,4},{14,6},{16,24},{18,... | collective-permute-start | bytes 4718600 | tf_op jit(solution)/shard_map/ppermute | solution.py:137
  147.2 0.0 all-to-all-done
  147.2 5.5 %copy.91 = bf16[2,96,16,384]{3,1,2,0:T(8,128)(2,1)} copy(bf16[2,96,16,384]{1,0,3,2:T(2,128)(2,1)S(1)} %bitcast.57) | data formatting | bytes 4718592 | tf_op jit(solution)/shard_map/all_to_all | solution.py:121
  152.7 0.0 all-gather.3.cloned.1.call-update
  152.7 0.0 all-gather.5.cloned.1.call-start
  152.8 28.6 %collective-permute-done.2 = bf16[512,1536]{0,1:T(8,128)(2,1)} collective-permute-done((bf16[512,1536]{0,1:T(8,128)(2,1)}, bf16[512,1536]{0,1:T(8,128)(2,1)}, u32[]{:S(2)}, u32[]{:S(2)}) %collective-permute-start.2) | collective-permute-done | bytes 1572896 | tf_op jit(solution)/shard_map/ppermute | solution.py:137
  181.4 4.1 maximum_select_fusion.1
  185.5 8.1 %collective-permute-start.3 = (bf16[1024,1536]{0,1:T(8,128)(2,1)S(1)}, bf16[1024,1536]{0,1:T(8,128)(2,1)}, u32[]{:S(2)}, u32[]{:S(2)}) collective-permute-start(bf16[1024,1536]{0,1:T(8,128)(2,1)S(1)} %maximum_select_fusion.1), channel_id=1, source_target_pairs={{0,16},{2,18},{4,20},{6,22},{8,24},{10,26},{12,28},{14,30},{16,0},... | collective-permute-start | bytes 9437192 | tf_op jit(solution)/shard_map/ppermute | solution.py:137
  193.6 1.4 copy.109
  195.0 159.3 %all_to_all.37 = bf16[16,384,96]{1,2,0:T(8,128)(2,1)} all-to-all(bf16[16,384,96]{1,2,0:T(8,128)(2,1)S(1)} %bitcast.61), channel_id=1, replica_groups=mesh['req'=16,'mlp'=2] {'req'}, dimensions={0} | all-to-all | bytes 2359296 | tf_op jit(solution)/shard_map/all_to_all | solution.py:123
  354.2 0.0 all-gather.5.cloned.1.call-update
  354.3 0.0 reduce-scatter.8.cloned.1.call-start
  354.3 0.0 collective-permute-done.3
  354.3 0.0 all-gather.3.cloned.1.call-done
  354.4 11.9 %fusion.10 = f32[2048,768]{1,0:T(8,128)} fusion(bf16[2,1536,768]{2,1,0:T(8,128)(2,1)} %all-gather.3.cloned.1.call-done, bf16[1024,1536]{0,1:T(8,128)(2,1)} %collective-permute-done.3, bf16[1024,1536]{0,1:T(8,128)(2,1)S(1)} %maximum_select_fusion.1, pred[]{:T(512)S(6)} %eq.28), kind=kOutput, calls=%fused_computation.17 | convolution fusion | flops 4860149760 | bytes 14942209 | tf_op jit(solution)/shard_map/dot_general | solution.py:144
  366.3 21.2 %convolution_convert_fusion = bf16[2048,1536]{1,0:T(8,128)(2,1)} fusion(bf16[768,1536]{0,1:T(8,128)(2,1)} %all-gather.5.cloned.1.call-done, f32[2048,768]{1,0:T(8,128)} %fusion.10, bf16[2,1536,768]{2,1,0:T(8,128)(2,1)} %all-gather.3.cloned.1.call-done, bf16[1024,1536]{0,1:T(8,128)(2,1)} %collective-permute-done.3, ...), kind=kOutput, calls=%fused_computation.8 | convolution fusion | flops 9704570880 | bytes 23592960 | tf_op jit(solution)/shard_map/dot_general | solution.py:146
  387.5 0.0 reduce-scatter.8.cloned.1.call-update
  387.5 1.1 copy-done
  388.6 0.3 copy.73
  388.9 145.4 %reduce-scatter.8.cloned.1.call-done = bf16[128,1536]{1,0:T(8,128)(2,1)} async-done(((bf16[2048,1536]{1,0:T(8,128)(2,1)}), bf16[128,1536]{1,0:T(8,128)(2,1)}) %reduce-scatter.8.cloned.1.call-update) | async-done | bytes 393232 | tf_op jit(solution)/shard_map/reduce_scatter | solution.py:147
  534.3 1.8 fusion.18
  (10 shorter events, 0.1 us)
Async XLA Ops:
  6.5 78.5 %reduce-scatter.10.cloned.1.call-start = ((), (), s32[]{:S(2)}) async-start(), calls=%async_computation.9 | async-start | bytes 196608
  7.9 7.0 %copy-start.2 = (bf16[1,128,512]{2,1,0:T(8,128)(2,1)S(1)}, bf16[1,128,512]{2,1,0:T(8,128)(2,1)}, u32[]{:S(2)}) copy-start(bf16[1,128,512]{2,1,0:T(8,128)(2,1)} %param.13) | copy-start | bytes 393220
  8.0 7.2 %copy-start.3 = (s32[16]{0:T(128)S(1)}, s32[16]{0:T(128)}, u32[]{:S(2)}) copy-start(s32[16]{0:T(128)} %param.16) | copy-start | bytes 196
  8.0 7.8 %copy-start.4 = (s32[16]{0:T(128)S(1)}, s32[16]{0:T(128)}, u32[]{:S(2)}) copy-start(s32[16]{0:T(128)} %param.15) | copy-start | bytes 196
  45.2 40.9 %reduce-scatter.6.cloned.1.call-start = ((), (), s32[]{:S(2)}) async-start(), calls=%async_computation.5 | async-start | bytes 2359296 | tf_op jit(solution)/shard_map/reduce_scatter | solution.py:126
  65.6 4.2 copy-start.1
  76.6 70.6 %all-to-all-start = ((bf16[2,96,6144]{1,0,2:T(2,128)(2,1)}), bf16[2,96,6144]{1,0,2:T(2,128)(2,1)S(1)}, u32[]{:S(2)}, u32[]{:S(2)}) async-start(bf16[2,96,6144]{1,0,2:T(2,128)(2,1)} %copy.69), calls=%async_computation.1 | async-start | bytes 6291456 | tf_op jit(solution)/shard_map/all_to_all | solution.py:121
  84.8 269.6 %all-gather.3.cloned.1.call-start = ((), (), s32[]{:S(2)}) async-start(), calls=%async_computation.6 | async-start | bytes 7077888 | tf_op jit(solution)/shard_map/all_gather | solution.py:122
  91.8 12.6 %collective-permute-start = (bf16[128,1536]{0,1:T(8,128)(2,1)S(1)}, bf16[128,1536]{0,1:T(8,128)(2,1)}, u32[]{:S(2)}, u32[]{:S(2)}) collective-permute-start(bf16[128,1536]{0,1:T(8,128)(2,1)S(1)} %multiply_convert_fusion.2), channel_id=1, source_target_pairs={{0,2},{2,0},{4,6},{6,4},{8,10},{10,8},{12,14},{14,12},{16,18},{18,... | collective-permute-start | bytes 1179656 | tf_op jit(solution)/shard_map/ppermute | solution.py:137
  106.6 31.5 %collective-permute-start.1 = (bf16[256,1536]{0,1:T(8,128)(2,1)}, bf16[256,1536]{0,1:T(8,128)(2,1)}, u32[]{:S(2)}, u32[]{:S(2)}) collective-permute-start(bf16[256,1536]{0,1:T(8,128)(2,1)} %maximum_select_fusion.5), channel_id=1, source_target_pairs={{0,4},{2,6},{4,0},{6,2},{8,12},{10,14},{12,8},{14,10},{16,20},{18,... | collective-permute-start | bytes 2359304 | tf_op jit(solution)/shard_map/ppermute | solution.py:137
  141.5 39.9 %collective-permute-start.2 = (bf16[512,1536]{0,1:T(8,128)(2,1)}, bf16[512,1536]{0,1:T(8,128)(2,1)}, u32[]{:S(2)}, u32[]{:S(2)}) collective-permute-start(bf16[512,1536]{0,1:T(8,128)(2,1)} %maximum_select_fusion.2), channel_id=1, source_target_pairs={{0,8},{2,10},{4,12},{6,14},{8,0},{10,2},{12,4},{14,6},{16,24},{18,... | collective-permute-start | bytes 4718600 | tf_op jit(solution)/shard_map/ppermute | solution.py:137
  152.7 213.5 %all-gather.5.cloned.1.call-start = ((), (), s32[]{:S(2)}) async-start(), calls=%async_computation.7 | async-start | bytes 3538944 | tf_op jit(solution)/shard_map/all_gather | solution.py:124
  185.5 168.8 %collective-permute-start.3 = (bf16[1024,1536]{0,1:T(8,128)(2,1)S(1)}, bf16[1024,1536]{0,1:T(8,128)(2,1)}, u32[]{:S(2)}, u32[]{:S(2)}) collective-permute-start(bf16[1024,1536]{0,1:T(8,128)(2,1)S(1)} %maximum_select_fusion.1), channel_id=1, source_target_pairs={{0,16},{2,18},{4,20},{6,22},{8,24},{10,26},{12,28},{14,30},{16,0},... | collective-permute-start | bytes 9437192 | tf_op jit(solution)/shard_map/ppermute | solution.py:137
  354.3 180.0 %reduce-scatter.8.cloned.1.call-start = ((), (), s32[]{:S(2)}) async-start(), calls=%async_computation.8 | async-start | bytes 6684672 | tf_op jit(solution)/shard_map/reduce_scatter | solution.py:147
  387.5 1.1 copy-start
Sparse Core Ops, SparseCore 0:
  45.3 10.0 reduce-scatter.9
  70.0 11.5 reduce-scatter.5
  152.8 23.2 all-gather.2
  354.4 11.7 all-gather.4
  387.6 146.6 reduce-scatter.7
